TPU v7x, 32 devices: a whole 2x2x4 slice. The times are simulated.
32 devices in a mesh: col: 4 (over z), row: 8 (over y, x, core).
Axes of the slice: x: 2, y: 2, z: 4, core: 2. Of those that a mesh axis runs over, the one named last changes fastest.
Arguments:
- affinity: bfloat16 [3840, 128, 128], P(('col', 'row')), may hold values from 0 to 0.015625
- tile_rows: int32 [3840], P(('col', 'row')), may hold values from 0 to 19
- tile_cols: int32 [3840], P(('col', 'row')), may hold values from 0 to 39
- live_tiles: int32 [32], P(('col', 'row')), may hold values from 1 to 120, as said below
- start: float32 [20480, 256], P(('col', 'row')), may hold values from -1500 to 1500
Outputs:
- vectors: float32 [20480, 256], P(('col', 'row'))
- first_passes: float32 [2, 20480, 256], P(None, ('col', 'row'))
Inputs may be any that keep to these rules, and one draw needn't show every extreme that they name: A device's tiles are its slots 0 to live_tiles - 1; later slots are ignored. Some device holds exactly 120 tiles.
All inputs are finite; a program needn't handle non-finite values.
Results may differ from a plain program's by a relative error of at most 0.0003.
Values sent between devices are 32-bit elements; how exact they have to be, the bound alone decides.
No kernel may reach another device: no remote copies, remote signals or barrier semaphores. Data moves between devices by JAX's collectives and lax.ppermute only.
A program may use at most 128 MiB of HBM per device.

v0:
```python
import jax
import jax.numpy as jnp
from jax import lax
from jax.sharding import PartitionSpec as P

ITERS = 2
highest = lax.Precision.HIGHEST


def local_gram(matrix):
    return jnp.dot(matrix.T, matrix, precision=highest, preferred_element_type=jnp.float32)


def inverse_lower(gram):
    lower = jnp.linalg.cholesky(gram)
    return jax.scipy.linalg.solve_triangular(
        lower, jnp.eye(gram.shape[0], dtype=jnp.float32), lower=True
    )


def apply_factor(matrix, inverse):
    return jnp.dot(matrix, inverse.T, precision=highest, preferred_element_type=jnp.float32)


def body(affinity, tile_rows, tile_cols, live_tiles, start):
    n_row = lax.axis_size("row")
    n_col = lax.axis_size("col")
    slot_count = affinity.shape[0]
    tile_size = affinity.shape[1]
    rows_local = start.shape[0]
    vec_count = start.shape[1]
    own_tiles = rows_local // tile_size
    live = (jnp.arange(slot_count) < live_tiles[0]).astype(jnp.float32)
    row_onehot = (jnp.arange(own_tiles * n_col)[:, None] == tile_rows[None, :]).astype(
        jnp.float32
    ) * live[None, :]
    row_sums = jnp.sum(affinity, axis=2, dtype=jnp.float32)
    degree_terms = jnp.dot(
        row_onehot, row_sums, precision=highest, preferred_element_type=jnp.float32
    )
    degree = 1.0 + lax.psum_scatter(degree_terms, "col", scatter_dimension=0, tiled=True).reshape(
        rows_local
    )
    scaling = (1.0 / jnp.sqrt(degree))[:, None]
    squares = affinity.astype(jnp.float32)
    firsts = []
    pending = start
    for step_number in range(ITERS):
        mapped_scaled = scaling * pending
        gathered = lax.all_gather(mapped_scaled, "row", axis=0, tiled=True)
        gathered = gathered.reshape(n_row * own_tiles, tile_size, vec_count)
        picked = gathered[tile_cols]
        products = jnp.einsum(
            "sij,sjk->sik", squares, picked, precision=highest, preferred_element_type=jnp.float32
        )
        terms = jnp.dot(
            row_onehot,
            products.reshape(slot_count, tile_size * vec_count),
            precision=highest,
            preferred_element_type=jnp.float32,
        )
        summed = lax.psum_scatter(terms, "col", scatter_dimension=0, tiled=True)
        raw_image = scaling * (mapped_scaled + summed.reshape(rows_local, vec_count))
        if step_number == 0:
            inner_gram = lax.psum(local_gram(raw_image), ("col", "row"))
            image_block = raw_image
        else:
            raw_gram, pending_gram = lax.psum(
                (local_gram(raw_image), local_gram(pending)), ("col", "row")
            )
            pending_inverse = inverse_lower(pending_gram)
            image_block = apply_factor(raw_image, pending_inverse)
            inner_gram = jnp.dot(
                jnp.dot(
                    pending_inverse, raw_gram, precision=highest, preferred_element_type=jnp.float32
                ),
                pending_inverse.T,
                precision=highest,
                preferred_element_type=jnp.float32,
            )
        pending = apply_factor(image_block, inverse_lower(inner_gram))
        firsts.append(pending)
    final_gram = lax.psum(local_gram(pending), ("col", "row"))
    basis = apply_factor(pending, inverse_lower(final_gram))
    total_images = rows_local * n_row * n_col
    root = jnp.sqrt(jnp.float32(total_images))
    return (root * basis, root * jnp.stack(firsts, axis=0))


def solution(mesh):
    placed = (
        P(("col", "row"), None, None),
        P(("col", "row")),
        P(("col", "row")),
        P(("col", "row")),
        P(("col", "row"), None),
    )
    return jax.shard_map(
        body,
        mesh=mesh,
        in_specs=placed,
        out_specs=(P(("col", "row"), None), P(None, ("col", "row"), None)),
        check_vma=False,
    )
```

profile of v0, /device:TPU:0, one launch (start us, length us, event | category | flops | bytes accessed | tf_op | source)
XLA Modules:
  0.0 1157.0 jit_solution(773065271221598994)
XLA Ops:
  7.9 3.2 convert_reduce_fusion
  11.9 20.4 %all-reduce.1 = f32[20,128]{1,0:T(8,128)S(1)} all-reduce(f32[20,128]{1,0:T(8,128)S(1)} %fusion.55), channel_id=2, replica_groups=mesh['col'=4,'row'=8] {'col'}, use_global_device_ids=true, to_apply=%region_1.0.clone | all-reduce | flops 2560 | bytes 20480
  32.4 1.4 fusion.81
  34.4 2.1 broadcast_multiply_fusion.1
  36.6 39.3 %all-gather.3.cloned.1.call-done = f32[5120,256]{1,0:T(8,128)} async-done(((f32[640,256]{1,0:T(8,128)}), f32[5120,256]{1,0:T(8,128)}) %all-gather.3.cloned.1.call-update) | async-done | bytes 5242896 | tf_op jit(solution)/shard_map/all_gather | solution.py:50
  75.9 12.1 %gather_fusion = f32[120,128,256]{2,1,0:T(8,128)} fusion(f32[40,128,256]{2,1,0:T(8,128)} %bitcast.166, s32[1024]{0:T(1024)S(1)} %pad_clamp_fusion), kind=kCustom, calls=%fused_computation | custom fusion | bytes 31457760 | tf_op jit(solution)/shard_map/gather | solution.py:52
  88.0 20.2 %convolution_bitcast_fusion.1 = f32[120,128,256]{1,2,0:T(8,128)} fusion(f32[120,128,256]{2,1,0:T(8,128)} %gather_fusion, bf16[120,128,128]{2,1,0:T(8,128)(2,1)} %param.8), kind=kOutput, calls=%fused_computation.11 | convolution fusion | flops 6039797760 | bytes 35389440 | tf_op jit(solution)/shard_map/sij,sjk->sik/dot_general | solution.py:53
  108.2 15.7 %copy.41 = f32[15,8,128,256]{3,1,2,0:T(8,128)} copy(f32[15,8,128,256]{2,3,1,0:T(8,128)} %bitcast.163) | data formatting | bytes 31457280
  123.9 10.5 fusion.53
  134.4 78.5 %fusion = f32[8,32768]{1,0:T(8,128)} fusion(f32[20,32768]{1,0:T(8,128)S(1)} %fusion.53), kind=kCustom, calls=%all-reduce-scatter | all-reduce-scatter fusion | flops 1048577 | bytes 3670528
  212.9 1.5 collective-permute-start
  214.4 1.3 slice.54
  215.7 2.6 collective-permute-start.1
  219.0 20.1 %collective-permute-done.1 = f32[1,32768]{1,0:T(1,128)S(1)} collective-permute-done((f32[1,32768]{1,0:T(1,128)S(1)}, f32[1,32768]{1,0:T(1,128)S(1)}, u32[]{:S(2)}, u32[]{:S(2)}) %collective-permute-start.1) | collective-permute-done | bytes 131104
  239.1 21.2 %concatenate.3 = f32[17,32768]{1,0:T(8,128)} concatenate(f32[1,32768]{1,0:T(1,128)S(1)} %collective-permute-done.1, f32[8,32768]{1,0:T(8,128)S(1)} %collective-permute-done, f32[8,32768]{1,0:T(8,128)} %fusion), dimensions={0} | concatenate | bytes 4456448
  260.3 1.7 constant_dynamic-slice_fusion.5
  262.4 2.2 fusion.29
  264.6 129.0 %all-reduce.11.cloned.1.call-done = f32[256,256]{0,1:T(8,128)} async-done(((f32[256,256]{0,1:T(8,128)}), f32[256,256]{0,1:T(8,128)}) %all-reduce.11.cloned.1.call-update) | async-done | bytes 262160 | tf_op jit(solution)/shard_map/psum | solution.py:65
  395.7 11.7 %cholesky.214 = f32[128,128]{1,0:T(8,128)S(1)} custom-call(f32[128,128]{1,0:T(8,128)S(1)} %cholesky.346), custom_call_target="Cholesky" | custom-call | tf_op jit(solution)/shard_map/jit(cholesky)/cholesky | solution.py:15
  407.5 9.8 custom-call.17
  417.8 11.7 %cholesky.231 = f32[128,128]{1,0:T(8,128)S(1)} custom-call(f32[128,128]{1,0:T(8,128)S(1)} %convolution_subtract_fusion.7), custom_call_target="Cholesky" | custom-call | tf_op jit(solution)/shard_map/jit(cholesky)/cholesky | solution.py:15
  431.8 15.1 %while.8 = (s32[]{:T(128)}, f32[256,256]{1,0:T(8,128)S(1)}, s32[2,2]{1,0:T(2,128)S(1)}, f32[2,128,128]{2,1,0:T(8,128)S(1)}, s32[]{:T(128)}) while((s32[]{:T(128)}, f32[256,256]{1,0:T(8,128)S(1)}, s32[2,2]{1,0:T(2,128)S(1)}, f32[2,128,128]{2,1,0:T(8,128)S(1)}, s32[]{:T(128)}) %tuple.83), condition=%wide.while_cond, body=%wide.while_body.sunk | while | flops 2 | bytes 131181 | solution.py:16
  443.4 1.4 bitcast_dynamic-update-slice_fusion.8
  445.5 1.4 bitcast_dynamic-update-slice_fusion.8
  446.9 19.7 %custom-call.18 = f32[2,128,128]{1,2,0:T(8,128)S(1)} custom-call(f32[2,128,128]{2,1,0:T(8,128)S(1)} %get-tuple-element.30), custom_call_target="InvertDiagBlocksLowerTriangular" | custom-call | tf_op jit(solution)/shard_map/jit(_solve_triangular)/triangular_solve | solution.py:16
  467.5 1.6 broadcast_multiply_fusion
  469.1 40.2 %all-gather.5.cloned.1.call-done = f32[5120,256]{1,0:T(8,128)} async-done(((f32[640,256]{1,0:T(8,128)}), f32[5120,256]{1,0:T(8,128)}) %all-gather.5.cloned.1.call-update) | async-done | bytes 5242896 | tf_op jit(solution)/shard_map/all_gather | solution.py:50
  509.3 12.1 %gather_fusion.1 = f32[120,128,256]{2,1,0:T(8,128)} fusion(f32[40,128,256]{2,1,0:T(8,128)} %bitcast.167, s32[1024]{0:T(1024)S(1)} %pad_clamp_fusion), kind=kCustom, calls=%fused_computation.1 | custom fusion | bytes 31457760 | tf_op jit(solution)/shard_map/gather | solution.py:52
  521.4 20.2 %convolution_bitcast_fusion = f32[120,128,256]{1,2,0:T(8,128)} fusion(f32[120,128,256]{2,1,0:T(8,128)} %gather_fusion.1, bf16[120,128,128]{2,1,0:T(8,128)(2,1)} %param.8), kind=kOutput, calls=%fused_computation.10 | convolution fusion | flops 6039797760 | bytes 35389440 | tf_op jit(solution)/shard_map/sij,sjk->sik/dot_general | solution.py:53
  541.6 15.7 %copy.42 = f32[15,8,128,256]{3,1,2,0:T(8,128)} copy(f32[15,8,128,256]{2,3,1,0:T(8,128)} %bitcast.165) | data formatting | bytes 31457280
  557.3 11.6 fusion.51
  568.9 78.6 %fusion.1 = f32[8,32768]{1,0:T(8,128)S(1)} fusion(f32[20,32768]{1,0:T(8,128)} %fusion.51), kind=kCustom, calls=%all-reduce-scatter.1 | all-reduce-scatter fusion | flops 1048577 | bytes 3670528
  647.4 2.3 collective-permute-start.2
  649.8 1.7 collective-permute-start.3
  651.5 1.9 fusion.82
  653.4 19.9 %collective-permute-done.3 = f32[1,32768]{1,0:T(1,128)S(1)} collective-permute-done((f32[1,32768]{1,0:T(1,128)S(1)}, f32[1,32768]{1,0:T(1,128)S(1)}, u32[]{:S(2)}, u32[]{:S(2)}) %collective-permute-start.3) | collective-permute-done | bytes 131104
  673.3 21.2 %concatenate.4 = f32[17,32768]{1,0:T(8,128)} concatenate(f32[1,32768]{1,0:T(1,128)S(1)} %collective-permute-done.3, f32[8,32768]{1,0:T(8,128)} %collective-permute-done.2, f32[8,32768]{1,0:T(8,128)S(1)} %fusion.1), dimensions={0} | concatenate | bytes 4456448
  694.5 1.7 constant_dynamic-slice_fusion.4
  696.6 2.1 fusion.30
  698.8 131.3 %all-reduce.15.cloned.1.call-done = (f32[256,256]{0,1:T(8,128)}, f32[256,256]{1,0:T(8,128)}) async-done(((f32[256,256]{0,1:T(8,128)}, f32[256,256]{1,0:T(8,128)}), (f32[256,256]{0,1:T(8,128)}, f32[256,256]{1,0:T(8,128)})) %all-reduce.15.cloned.1.call-update) | async-done | bytes 524304 | tf_op jit(solution)/shard_map/psum | solution.py:68
  832.2 11.7 %cholesky.248 = f32[128,128]{1,0:T(8,128)S(1)} custom-call(f32[128,128]{1,0:T(8,128)S(1)} %cholesky.349), custom_call_target="Cholesky" | custom-call | tf_op jit(solution)/shard_map/jit(cholesky)/cholesky | solution.py:15
  844.0 9.8 custom-call.19
  854.3 11.7 %cholesky.265 = f32[128,128]{1,0:T(8,128)S(1)} custom-call(f32[128,128]{1,0:T(8,128)S(1)} %convolution_subtract_fusion.6), custom_call_target="Cholesky" | custom-call | tf_op jit(solution)/shard_map/jit(cholesky)/cholesky | solution.py:15
  868.7 4.0 while.9
  869.3 1.4 bitcast_dynamic-update-slice_fusion.9
  871.3 1.4 bitcast_dynamic-update-slice_fusion.9
  872.7 19.8 %custom-call.20 = f32[2,128,128]{1,2,0:T(8,128)S(1)} custom-call(f32[2,128,128]{2,1,0:T(8,128)S(1)} %get-tuple-element.31), custom_call_target="InvertDiagBlocksLowerTriangular" | custom-call | tf_op jit(solution)/shard_map/jit(_solve_triangular)/triangular_solve | solution.py:16
  895.2 11.7 %cholesky.282 = f32[128,128]{1,0:T(8,128)S(1)} custom-call(f32[128,128]{1,0:T(8,128)S(1)} %cholesky.352), custom_call_target="Cholesky" | custom-call | tf_op jit(solution)/shard_map/jit(cholesky)/cholesky | solution.py:15
  907.0 9.8 custom-call.21
  917.3 11.9 %cholesky.299 = f32[128,128]{1,0:T(8,128)S(1)} custom-call(f32[128,128]{1,0:T(8,128)S(1)} %convolution_subtract_fusion.5), custom_call_target="Cholesky" | custom-call | tf_op jit(solution)/shard_map/jit(cholesky)/cholesky | solution.py:15
  931.8 4.0 while.10
  932.4 1.4 bitcast_dynamic-update-slice_fusion.10
  934.5 1.4 bitcast_dynamic-update-slice_fusion.10
  935.8 19.7 %custom-call.22 = f32[2,128,128]{1,2,0:T(8,128)S(1)} custom-call(f32[2,128,128]{2,1,0:T(8,128)S(1)} %get-tuple-element.32), custom_call_target="InvertDiagBlocksLowerTriangular" | custom-call | tf_op jit(solution)/shard_map/jit(_solve_triangular)/triangular_solve | solution.py:16
  957.2 1.9 fusion.83
  960.3 124.6 %all-reduce.13.cloned.1.call-done = f32[256,256]{0,1:T(8,128)} async-done(((f32[256,256]{0,1:T(8,128)}), f32[256,256]{0,1:T(8,128)}) %all-reduce.13.cloned.1.call-update) | async-done | bytes 262160 | tf_op jit(solution)/shard_map/psum | solution.py:83
  1087.0 11.7 %cholesky.316 = f32[128,128]{1,0:T(8,128)S(1)} custom-call(f32[128,128]{1,0:T(8,128)S(1)} %cholesky.355), custom_call_target="Cholesky" | custom-call | tf_op jit(solution)/shard_map/jit(cholesky)/cholesky | solution.py:15
  1098.8 9.8 custom-call.23
  1109.1 11.9 %cholesky.333 = f32[128,128]{1,0:T(8,128)S(1)} custom-call(f32[128,128]{1,0:T(8,128)S(1)} %convolution_subtract_fusion.4), custom_call_target="Cholesky" | custom-call | tf_op jit(solution)/shard_map/jit(cholesky)/cholesky | solution.py:15
  1123.8 4.1 while.11
  1124.4 1.4 bitcast_dynamic-update-slice_fusion.11
  1126.5 1.4 bitcast_dynamic-update-slice_fusion.11
  1127.9 19.7 %custom-call.24 = f32[2,128,128]{1,2,0:T(8,128)S(1)} custom-call(f32[2,128,128]{2,1,0:T(8,128)S(1)} %get-tuple-element.33), custom_call_target="InvertDiagBlocksLowerTriangular" | custom-call | tf_op jit(solution)/shard_map/jit(_solve_triangular)/triangular_solve | solution.py:16
  1148.5 1.6 convolution_multiply_fusion
  (111 shorter events, 27.2 us)
Async XLA Ops:
  7.2 29.4 %copy-start.3 = (s32[120]{0:T(128)S(1)}, s32[120]{0:T(128)}, u32[]{:S(2)}) copy-start(s32[120]{0:T(128)} %param.10) | copy-start | bytes 1444
  7.2 68.7 %all-gather.3.cloned.1.call-start = ((), (), s32[]{:S(2)}) async-start(), calls=%async_computation | async-start | bytes 5898240 | tf_op jit(solution)/shard_map/all_gather | solution.py:50
  36.5 357.1 %all-reduce.11.cloned.1.call-start = ((), (), s32[]{:S(2)}) async-start(), calls=%async_computation.1 | async-start | bytes 524288 | tf_op jit(solution)/shard_map/psum | solution.py:65
  108.2 15.7 %copy-start.2 = (s32[120]{0:T(128)S(1)}, s32[120]{0:T(128)}, u32[]{:S(2)}) copy-start(s32[120]{0:T(128)} %param.9) | copy-start | bytes 1444
  212.9 49.5 %copy-start = (f32[640,256]{1,0:T(8,128)S(1)}, f32[640,256]{1,0:T(8,128)}, u32[]{:S(2)}) copy-start(f32[640,256]{1,0:T(8,128)} %param.12) | copy-start | bytes 1966084
  212.9 26.2 %collective-permute-start = (f32[8,32768]{1,0:T(8,128)}, f32[8,32768]{1,0:T(8,128)S(1)}, u32[]{:S(2)}, u32[]{:S(2)}) collective-permute-start(f32[8,32768]{1,0:T(8,128)} %fusion), channel_id=1, source_target_pairs={{0,8},{8,16},{16,24},{1,9},{9,17},{17,25},{2,10},{10,18},{18,26},{... | collective-permute-start | bytes 3145736
  215.7 23.4 %collective-permute-start.1 = (f32[1,32768]{1,0:T(1,128)S(1)}, f32[1,32768]{1,0:T(1,128)S(1)}, u32[]{:S(2)}, u32[]{:S(2)}) collective-permute-start(f32[1,32768]{1,0:T(1,128)S(1)} %slice.54), channel_id=1, source_target_pairs={{0,16},{8,24},{1,17},{9,25},{2,18},{10,26},{3,19},{11,27},{4,20},{... | collective-permute-start | bytes 393224
  264.6 244.7 %all-gather.5.cloned.1.call-start = ((), (), s32[]{:S(2)}) async-start(), calls=%async_computation.2 | async-start | bytes 5898240 | tf_op jit(solution)/shard_map/all_gather | solution.py:50
  469.1 361.0 %all-reduce.15.cloned.1.call-start = ((), (), s32[]{:S(2)}) async-start(), calls=%async_computation.4 | async-start | bytes 1048576 | tf_op jit(solution)/shard_map/psum | solution.py:68
  647.4 25.9 %collective-permute-start.2 = (f32[8,32768]{1,0:T(8,128)S(1)}, f32[8,32768]{1,0:T(8,128)}, u32[]{:S(2)}, u32[]{:S(2)}) collective-permute-start(f32[8,32768]{1,0:T(8,128)S(1)} %fusion.1), channel_id=1, source_target_pairs={{0,8},{8,16},{16,24},{1,9},{9,17},{17,25},{2,10},{10,18},{18,26},{... | collective-permute-start | bytes 3145736
  649.8 23.5 %collective-permute-start.3 = (f32[1,32768]{1,0:T(1,128)S(1)}, f32[1,32768]{1,0:T(1,128)S(1)}, u32[]{:S(2)}, u32[]{:S(2)}) collective-permute-start(f32[1,32768]{1,0:T(1,128)S(1)} %slice.55), channel_id=1, source_target_pairs={{0,16},{8,24},{1,17},{9,25},{2,18},{10,26},{3,19},{11,27},{4,20},{... | collective-permute-start | bytes 393224
  698.7 386.2 %all-reduce.13.cloned.1.call-start = ((), (), s32[]{:S(2)}) async-start(), calls=%async_computation.3 | async-start | bytes 524288 | tf_op jit(solution)/shard_map/psum | solution.py:83
  830.1 64.1 %copy-start.1 = (f32[256,256]{1,0:T(8,128)S(1)}, f32[256,256]{1,0:T(8,128)}, u32[]{:S(2)}) copy-start(f32[256,256]{1,0:T(8,128)} %get-tuple-element.67) | copy-start | bytes 786436
Sparse Core Ops, SparseCore 0:
  36.7 39.1 all-gather.2
  264.7 128.9 all-reduce.10
  469.2 40.0 all-gather.4
  698.9 131.1 all-reduce.14
  959.2 125.6 all-reduce.12
where the time goes:
time: 1170 us; the launch traced here: 1160 us
  waiting for transfers between devices  504 us (43%)
  other arithmetic  227 us (19%)
  blocking collectives  177 us (15%)
  local copies, waits for them, and re-layouts  125 us (11%)
  matrix products  82.1 us (7%)
  between operations  22.1 us (2%)
    unnamed x3, blocking collectives  177 us
    another operation x27, other arithmetic, inverse_lower(): lower = jnp.linalg.cholesky(gram)  138 us
    psum x1, waiting for transfers between devices, body(): lax.psum((local_gram(raw_image), local_gram(pending)), ('col', 'row'))  131 us
    psum x1, waiting for transfers between devices, body(): inner_gram = lax.psum(local_gram(raw_image), ('col', 'row'))  129 us
    psum x1, waiting for transfers between devices, body(): final_gram = lax.psum(local_gram(pending), ('col', 'row'))  125 us
    unnamed x17, local copies, waits for them, and re-layouts  80.2 us
    all_gather x2, waiting for transfers between devices, body(): gathered = lax.all_gather(mapped_scaled, 'row', axis=0, tiled=True)  79.4 us
    another operation x9, other arithmetic, inverse_lower(): jax.scipy.linalg.solve_triangular(lower, jnp.eye(gram.shape[0], dtype=jnp...  79 us
  transfers between devices with their start and end apart: 9, of which 7 were waited for; matrix products, arithmetic and copies ran while one was open for 0% of the time, Pallas kernels for 0%

commit v1 on v0

--- a/solution.py
+++ b/solution.py
@@ -47,7 +47,8 @@
     pending = start
     for step_number in range(ITERS):
         mapped_scaled = scaling * pending
-        gathered = lax.all_gather(mapped_scaled, "row", axis=0, tiled=True)
+        sent = jnp.stack([mapped_scaled] * lax.axis_size("row"))
+        gathered = jnp.concatenate(lax.all_to_all(sent, "row", 0, 0), axis=0)
         gathered = gathered.reshape(n_row * own_tiles, tile_size, vec_count)
         picked = gathered[tile_cols]
         products = jnp.einsum(

time: 1170 us -> 1200 us (1.026)
  blocking collectives: 177 us -> 233 us
  waiting for transfers between devices: 504 us -> 488 us
    all_gather x2 -> x0, waiting for transfers between devices: 79.4 us -> none  [body(): gathered = lax.all_gather(mapped_scaled, 'row', axis=0, tiled=True)]
    all_to_all x0 -> x1, blocking collectives: none -> 63.8 us  [body(): gathered = jnp.concatenate(lax.all_to_all(sent, 'row', 0, 0), axis=0)]
    all_to_all x0 -> x1, waiting for transfers between devices: none -> 60.1 us  [body(): gathered = jnp.concatenate(lax.all_to_all(sent, 'row', 0, 0), axis=0)]
    unnamed x9 -> x7, waiting for transfers between devices: 40 us -> 36.2 us
  transfers between devices with their start and end apart: 9 -> 8, of which waited for: 7 -> 6; matrix products, arithmetic and copies ran while one was open for 0% -> 0% of each run, Pallas kernels for 0% -> 0%
where the time goes in v1:
time: 1200 us; the launch traced here: 1190 us
  waiting for transfers between devices  488 us (41%)
  blocking collectives  233 us (19%)
  other arithmetic  226 us (19%)
  local copies, waits for them, and re-layouts  128 us (11%)
  matrix products  81.3 us (7%)
  between operations  21.9 us (2%)
  starting transfers between devices  13.8 us (1%)
    unnamed x3, blocking collectives  169 us
    another operation x27, other arithmetic, inverse_lower(): lower = jnp.linalg.cholesky(gram)  138 us
    psum x1, waiting for transfers between devices, body(): inner_gram = lax.psum(local_gram(raw_image), ('col', 'row'))  135 us
    psum x1, waiting for transfers between devices, body(): lax.psum((local_gram(raw_image), local_gram(pending)), ('col', 'row'))  133 us
    psum x1, waiting for transfers between devices, body(): final_gram = lax.psum(local_gram(pending), ('col', 'row'))  125 us
    unnamed x17, local copies, waits for them, and re-layouts  80.1 us
    another operation x9, other arithmetic, inverse_lower(): jax.scipy.linalg.solve_triangular(lower, jnp.eye(gram.shape[0], dtype=jnp...  79 us
    all_to_all x1, blocking collectives, body(): gathered = jnp.concatenate(lax.all_to_all(sent, 'row', 0, 0), axis=0)  63.8 us
  transfers between devices with their start and end apart: 8, of which 6 were waited for; matrix products, arithmetic and copies ran while one was open for 0% of the time, Pallas kernels for 0%

profile of v1, /device:TPU:0, one launch (start us, length us, event | category | flops | bytes accessed | tf_op | source)
XLA Modules:
  0.0 1192.6 jit_solution(5159537698940306170)
XLA Ops:
  7.8 3.2 convert_reduce_fusion
  11.9 20.4 %all-reduce.1 = f32[20,128]{1,0:T(8,128)S(1)} all-reduce(f32[20,128]{1,0:T(8,128)S(1)} %fusion.55), channel_id=2, replica_groups=mesh['col'=4,'row'=8] {'col'}, use_global_device_ids=true, to_apply=%region_1.0.clone | all-reduce | flops 2560 | bytes 20480
  32.3 1.3 fusion.81
  35.5 2.8 stack.10
  38.3 4.8 all-to-all-start
  43.3 60.1 %all-to-all-done = f32[8,640,256]{2,1,0:T(8,128)} async-done(((f32[8,640,256]{2,1,0:T(8,128)}), f32[8,640,256]{2,1,0:T(8,128)}, u32[]{:S(2)}, u32[]{:S(2)}) %all-to-all-start) | async-done | bytes 5242912 | tf_op jit(solution)/shard_map/all_to_all | solution.py:51
  103.4 12.1 %gather_fusion = f32[120,128,256]{2,1,0:T(8,128)} fusion(f32[40,128,256]{2,1,0:T(8,128)} %bitcast.2, s32[1024]{0:T(1024)S(1)} %pad_clamp_fusion), kind=kCustom, calls=%fused_computation | custom fusion | bytes 31457760 | tf_op jit(solution)/shard_map/gather | solution.py:53
  115.6 20.2 %convolution_bitcast_fusion.1 = f32[120,128,256]{1,2,0:T(8,128)} fusion(f32[120,128,256]{2,1,0:T(8,128)} %gather_fusion, bf16[120,128,128]{2,1,0:T(8,128)(2,1)} %param.8), kind=kOutput, calls=%fused_computation.11 | convolution fusion | flops 6039797760 | bytes 35389440 | tf_op jit(solution)/shard_map/sij,sjk->sik/dot_general | solution.py:54
  135.7 15.7 %copy.41 = f32[15,8,128,256]{3,1,2,0:T(8,128)} copy(f32[15,8,128,256]{2,3,1,0:T(8,128)} %bitcast.164) | data formatting | bytes 31457280
  151.5 10.5 fusion.53
  161.9 72.8 %fusion = f32[8,32768]{1,0:T(8,128)} fusion(f32[20,32768]{1,0:T(8,128)S(1)} %fusion.53), kind=kCustom, calls=%all-reduce-scatter | all-reduce-scatter fusion | flops 1048577 | bytes 3670528
  234.8 1.5 collective-permute-start
  236.2 1.3 slice.54
  237.6 2.6 collective-permute-start.1
  240.8 17.3 %collective-permute-done.1 = f32[1,32768]{1,0:T(1,128)S(1)} collective-permute-done((f32[1,32768]{1,0:T(1,128)S(1)}, f32[1,32768]{1,0:T(1,128)S(1)}, u32[]{:S(2)}, u32[]{:S(2)}) %collective-permute-start.1) | collective-permute-done | bytes 131104
  258.1 21.2 %concatenate.3 = f32[17,32768]{1,0:T(8,128)} concatenate(f32[1,32768]{1,0:T(1,128)S(1)} %collective-permute-done.1, f32[8,32768]{1,0:T(8,128)S(1)} %collective-permute-done, f32[8,32768]{1,0:T(8,128)} %fusion), dimensions={0} | concatenate | bytes 4456448
  279.3 1.7 constant_dynamic-slice_fusion.5
  281.4 2.2 fusion.29
  283.6 134.5 %all-reduce.11.cloned.1.call-done = f32[256,256]{0,1:T(8,128)} async-done(((f32[256,256]{0,1:T(8,128)}), f32[256,256]{0,1:T(8,128)}) %all-reduce.11.cloned.1.call-update) | async-done | bytes 262160 | tf_op jit(solution)/shard_map/psum | solution.py:66
  420.3 11.7 cholesky.214
  432.0 9.8 custom-call.17
  442.3 11.7 cholesky.231
  456.3 4.3 while.8
  457.1 1.4 bitcast_dynamic-update-slice_fusion.8
  459.1 1.4 bitcast_dynamic-update-slice_fusion.8
  460.6 19.7 %custom-call.18 = f32[2,128,128]{1,2,0:T(8,128)S(1)} custom-call(f32[2,128,128]{2,1,0:T(8,128)S(1)} %get-tuple-element.30), custom_call_target="InvertDiagBlocksLowerTriangular" | custom-call | tf_op jit(solution)/shard_map/jit(_solve_triangular)/triangular_solve | solution.py:16
  482.4 63.8 %all_to_all.10 = f32[8,640,256]{2,1,0:T(8,128)} all-to-all(f32[8,640,256]{2,1,0:T(8,128)S(1)} %stack.11), channel_id=1, replica_groups=mesh['col'=4,'row'=8] {'row'}, dimensions={0} | all-to-all | bytes 10485760 | tf_op jit(solution)/shard_map/all_to_all | solution.py:51
  546.2 12.1 %gather_fusion.1 = f32[120,128,256]{2,1,0:T(8,128)} fusion(f32[40,128,256]{2,1,0:T(8,128)} %bitcast.162, s32[1024]{0:T(1024)S(1)} %pad_clamp_fusion), kind=kCustom, calls=%fused_computation.1 | custom fusion | bytes 31457760 | tf_op jit(solution)/shard_map/gather | solution.py:53
  558.3 20.2 %convolution_bitcast_fusion = f32[120,128,256]{1,2,0:T(8,128)} fusion(f32[120,128,256]{2,1,0:T(8,128)} %gather_fusion.1, bf16[120,128,128]{2,1,0:T(8,128)(2,1)} %param.8), kind=kOutput, calls=%fused_computation.10 | convolution fusion | flops 6039797760 | bytes 35389440 | tf_op jit(solution)/shard_map/sij,sjk->sik/dot_general | solution.py:54
  578.5 15.7 %copy.42 = f32[15,8,128,256]{3,1,2,0:T(8,128)} copy(f32[15,8,128,256]{2,3,1,0:T(8,128)} %bitcast.166) | data formatting | bytes 31457280
  594.2 11.6 fusion.51
  605.8 76.1 %fusion.1 = f32[8,32768]{1,0:T(8,128)S(1)} fusion(f32[20,32768]{1,0:T(8,128)} %fusion.51), kind=kCustom, calls=%all-reduce-scatter.1 | all-reduce-scatter fusion | flops 1048577 | bytes 3670528
  681.8 3.0 collective-permute-start.2
  684.9 1.6 collective-permute-start.3
  686.6 1.9 fusion.82
  688.5 18.9 %collective-permute-done.3 = f32[1,32768]{1,0:T(1,128)S(1)} collective-permute-done((f32[1,32768]{1,0:T(1,128)S(1)}, f32[1,32768]{1,0:T(1,128)S(1)}, u32[]{:S(2)}, u32[]{:S(2)}) %collective-permute-start.3) | collective-permute-done | bytes 131104
  707.4 21.2 %concatenate.4 = f32[17,32768]{1,0:T(8,128)} concatenate(f32[1,32768]{1,0:T(1,128)S(1)} %collective-permute-done.3, f32[8,32768]{1,0:T(8,128)} %collective-permute-done.2, f32[8,32768]{1,0:T(8,128)S(1)} %fusion.1), dimensions={0} | concatenate | bytes 4456448
  728.6 1.7 constant_dynamic-slice_fusion.4
  730.6 2.1 fusion.30
  732.9 133.0 %all-reduce.15.cloned.1.call-done = (f32[256,256]{0,1:T(8,128)}, f32[256,256]{1,0:T(8,128)}) async-done(((f32[256,256]{0,1:T(8,128)}, f32[256,256]{1,0:T(8,128)}), (f32[256,256]{0,1:T(8,128)}, f32[256,256]{1,0:T(8,128)})) %all-reduce.15.cloned.1.call-update) | async-done | bytes 524304 | tf_op jit(solution)/shard_map/psum | solution.py:69
  868.0 11.7 cholesky.248
  879.7 9.8 custom-call.19
  890.0 11.7 cholesky.265
  904.4 4.0 while.9
  905.0 1.4 bitcast_dynamic-update-slice_fusion.9
  907.0 1.4 bitcast_dynamic-update-slice_fusion.9
  908.4 19.8 %custom-call.20 = f32[2,128,128]{1,2,0:T(8,128)S(1)} custom-call(f32[2,128,128]{2,1,0:T(8,128)S(1)} %get-tuple-element.31), custom_call_target="InvertDiagBlocksLowerTriangular" | custom-call | tf_op jit(solution)/shard_map/jit(_solve_triangular)/triangular_solve | solution.py:16
  931.0 11.7 cholesky.282
  942.7 9.8 custom-call.21
  953.0 11.9 cholesky.299
  967.6 4.0 while.10
  968.2 1.4 bitcast_dynamic-update-slice_fusion.10
  970.2 1.4 bitcast_dynamic-update-slice_fusion.10
  971.6 19.7 %custom-call.22 = f32[2,128,128]{1,2,0:T(8,128)S(1)} custom-call(f32[2,128,128]{2,1,0:T(8,128)S(1)} %get-tuple-element.32), custom_call_target="InvertDiagBlocksLowerTriangular" | custom-call | tf_op jit(solution)/shard_map/jit(_solve_triangular)/triangular_solve | solution.py:16
  992.9 1.9 fusion.83
  996.0 124.6 %all-reduce.13.cloned.1.call-done = f32[256,256]{0,1:T(8,128)} async-done(((f32[256,256]{0,1:T(8,128)}), f32[256,256]{0,1:T(8,128)}) %all-reduce.13.cloned.1.call-update) | async-done | bytes 262160 | tf_op jit(solution)/shard_map/psum | solution.py:84
  1122.7 11.7 cholesky.316
  1134.5 9.8 custom-call.23
  1144.8 11.9 %cholesky.333 = f32[128,128]{1,0:T(8,128)S(1)} custom-call(f32[128,128]{1,0:T(8,128)S(1)} %convolution_subtract_fusion.4), custom_call_target="Cholesky" | custom-call | tf_op jit(solution)/shard_map/jit(cholesky)/cholesky | solution.py:15
  1159.5 4.1 while.11
  1160.2 1.4 bitcast_dynamic-update-slice_fusion.11
  1162.2 1.4 bitcast_dynamic-update-slice_fusion.11
  1163.7 19.7 %custom-call.24 = f32[2,128,128]{1,2,0:T(8,128)S(1)} custom-call(f32[2,128,128]{2,1,0:T(8,128)S(1)} %get-tuple-element.33), custom_call_target="InvertDiagBlocksLowerTriangular" | custom-call | tf_op jit(solution)/shard_map/jit(_solve_triangular)/triangular_solve | solution.py:16
  1184.2 1.6 convolution_multiply_fusion
  (110 shorter events, 29.7 us)
Async XLA Ops:
  38.3 5.0 copy-start.3
  38.3 65.1 %all-to-all-start = ((f32[8,640,256]{2,1,0:T(8,128)}), f32[8,640,256]{2,1,0:T(8,128)}, u32[]{:S(2)}, u32[]{:S(2)}) async-start(f32[8,640,256]{2,1,0:T(8,128)} %stack.10), calls=%async_computation | async-start | bytes 10485760 | tf_op jit(solution)/shard_map/all_to_all | solution.py:51
  43.1 375.1 %all-reduce.11.cloned.1.call-start = ((), (), s32[]{:S(2)}) async-start(), calls=%async_computation.2 | async-start | bytes 524288 | tf_op jit(solution)/shard_map/psum | solution.py:66
  135.7 15.7 %copy-start.2 = (s32[120]{0:T(128)S(1)}, s32[120]{0:T(128)}, u32[]{:S(2)}) copy-start(s32[120]{0:T(128)} %param.9) | copy-start | bytes 1444
  234.8 46.6 %copy-start = (f32[640,256]{1,0:T(8,128)S(1)}, f32[640,256]{1,0:T(8,128)}, u32[]{:S(2)}) copy-start(f32[640,256]{1,0:T(8,128)} %param.12) | copy-start | bytes 1966084
  234.8 23.3 %collective-permute-start = (f32[8,32768]{1,0:T(8,128)}, f32[8,32768]{1,0:T(8,128)S(1)}, u32[]{:S(2)}, u32[]{:S(2)}) collective-permute-start(f32[8,32768]{1,0:T(8,128)} %fusion), channel_id=1, source_target_pairs={{0,8},{8,16},{16,24},{1,9},{9,17},{17,25},{2,10},{10,18},{18,26},{... | collective-permute-start | bytes 3145736
  237.6 20.5 %collective-permute-start.1 = (f32[1,32768]{1,0:T(1,128)S(1)}, f32[1,32768]{1,0:T(1,128)S(1)}, u32[]{:S(2)}, u32[]{:S(2)}) collective-permute-start(f32[1,32768]{1,0:T(1,128)S(1)} %slice.54), channel_id=1, source_target_pairs={{0,16},{8,24},{1,17},{9,25},{2,18},{10,26},{3,19},{11,27},{4,20},{... | collective-permute-start | bytes 393224
  283.6 582.3 %all-reduce.15.cloned.1.call-start = ((), (), s32[]{:S(2)}) async-start(), calls=%async_computation.4 | async-start | bytes 1048576 | tf_op jit(solution)/shard_map/psum | solution.py:69
  681.8 25.6 %collective-permute-start.2 = (f32[8,32768]{1,0:T(8,128)S(1)}, f32[8,32768]{1,0:T(8,128)}, u32[]{:S(2)}, u32[]{:S(2)}) collective-permute-start(f32[8,32768]{1,0:T(8,128)S(1)} %fusion.1), channel_id=1, source_target_pairs={{0,8},{8,16},{16,24},{1,9},{9,17},{17,25},{2,10},{10,18},{18,26},{... | collective-permute-start | bytes 3145736
  684.9 22.4 %collective-permute-start.3 = (f32[1,32768]{1,0:T(1,128)S(1)}, f32[1,32768]{1,0:T(1,128)S(1)}, u32[]{:S(2)}, u32[]{:S(2)}) collective-permute-start(f32[1,32768]{1,0:T(1,128)S(1)} %slice.55), channel_id=1, source_target_pairs={{0,16},{8,24},{1,17},{9,25},{2,18},{10,26},{3,19},{11,27},{4,20},{... | collective-permute-start | bytes 393224
  732.8 387.9 %all-reduce.13.cloned.1.call-start = ((), (), s32[]{:S(2)}) async-start(), calls=%async_computation.3 | async-start | bytes 524288 | tf_op jit(solution)/shard_map/psum | solution.py:84
  865.8 64.1 %copy-start.1 = (f32[256,256]{1,0:T(8,128)S(1)}, f32[256,256]{1,0:T(8,128)}, u32[]{:S(2)}) copy-start(f32[256,256]{1,0:T(8,128)} %get-tuple-element.67) | copy-start | bytes 786436
Sparse Core Ops, SparseCore 0:
  283.7 134.4 all-reduce.10
  732.9 132.8 all-reduce.14
  995.0 125.6 all-reduce.12
